TPU v7x, 32 devices: a whole 2x2x4 slice. The times are simulated.
32 devices in a mesh: seq: 8 (over y, x, core), req: 4 (over z).
Axes of the slice: x: 2, y: 2, z: 4, core: 2. Of those that a mesh axis runs over, the one named last changes fastest.
Arguments:
- queries: bfloat16 [8, 256, 1536], P('req', 'seq'), as said below
- new_kv: bfloat16 [2, 8, 256, 512], P(None, 'req', 'seq'), may hold values from -6 to 6
- cache_kv: bfloat16 [2, 8, 2048, 512], P(None, 'req', 'seq'), as said below
- cache_spans: int32 [8, 2], P('req'), may hold values from 0 to 2048, as said below
- recompute_rows: int32 [8, 256], P('req'), may hold values from 0 to 2047, as said below
- held_states: bfloat16 [8, 256, 1536], P('req', 'seq'), may hold values from -6 to 6
- key_weight: bfloat16 [1536, 512], replicated, may hold values from -0.15625 to 0.15625
- norm_gain: float32 [1536], replicated, may hold values from 0.1 to 1.9
- routes: int32 [8, 256, 8], P('req', 'seq'), may hold values from 0 to 19, all different within a row; in each aligned block of 32 rows (0 to 31, 32 to 63, ..., all dimensions but the last counted through in order) at most 16 rows name the same one
- route_weights: float32 [8, 256, 8], P('req', 'seq'), may hold values from 0.05 to 1
- expert_gate_up: bfloat16 [20, 1536, 1024], P('req'), may hold values from -0.15625 to 0.15625
- expert_down: bfloat16 [20, 512, 1536], P('req'), may hold values from -0.25 to 0.25
Outputs:
- layer_out: bfloat16 [8, 256, 1536], P('req', 'seq')
Inputs may be any that keep to these rules, and one draw needn't show every extreme that they name: `routes`: in each aligned block of 32 rows of one request (one device's rows of that request) no expert is named more than 16 times. cache_spans[r] = (start, length): 1024 <= length <= 2048 with some request of length 2048; 0 <= start <= 512 with some request starting at 0. `recompute_rows`: within a request the rows are distinct and lie between the request's start and length. `queries`: entries lie within -6 to 6. `cache_kv`: entries lie within -6 to 6.
All inputs are finite; a program needn't handle non-finite values.
Results may differ from a plain program's by a relative error of at most 0.034.
Values may be sent and summed in bfloat16 or wider, within the bound.
A program may use at most 192 MiB of HBM per device.

v0:
```python
import jax
import jax.numpy as jnp
from jax import lax
from jax.sharding import PartitionSpec as P

H = 24
KVH = 8
HD = 64
FF = 512
TOP = 8
CAP = 16
NEG = -1e30
THETA = 10000.0


def rotate(key_heads, positions):
    half_dim = key_heads.shape[-1] // 2
    exponent = jnp.arange(half_dim).astype(jnp.float32) * (2.0 / key_heads.shape[-1])
    inverse = THETA ** (-exponent)
    angles = positions.astype(jnp.float32)[..., None] * inverse
    cosine = jnp.cos(angles)[..., None, :]
    sine_part = jnp.sin(angles)[..., None, :]
    lower_half = key_heads[..., :half_dim]
    upper_half = key_heads[..., half_dim:]
    return jnp.concatenate(
        [
            lower_half * cosine - upper_half * sine_part,
            upper_half * cosine + lower_half * sine_part,
        ],
        axis=-1,
    )


def partial_attend(packed):
    query_rows, key_rows, value_rows, allowed = packed
    query_count, model_width = query_rows.shape
    key_count = key_rows.shape[0]
    groups = H // KVH
    query_heads = query_rows.reshape(query_count, KVH, groups, HD)
    key_heads = key_rows.reshape(key_count, KVH, HD)
    value_heads = value_rows.reshape(key_count, KVH, HD)
    scores = jnp.einsum(
        "qkgd,nkd->kgqn", query_heads, key_heads, preferred_element_type=jnp.float32
    ) * HD ** (-0.5)
    scores = jnp.where(allowed[None, None, :, :], scores, NEG)
    highest = jnp.max(scores, axis=-1, keepdims=True)
    exps = jnp.exp(scores - highest)
    totals = jnp.sum(exps, axis=-1)
    weights = exps.astype(jnp.bfloat16)
    mixed_rows = jnp.einsum(
        "kgqn,nkd->qkgd", weights, value_heads, preferred_element_type=jnp.float32
    )
    mixed_rows = mixed_rows / jnp.transpose(totals, (2, 0, 1))[..., None]
    log_total = highest[..., 0] + jnp.log(totals)
    log_rows = jnp.transpose(log_total, (2, 0, 1)).reshape(query_count, H)
    return (mixed_rows.reshape(query_count, model_width), log_rows)


def body(
    queries,
    new_kv,
    cache_kv,
    cache_spans,
    recompute_rows,
    held_states,
    key_weight,
    norm_gain,
    routes,
    route_weights,
    expert_gate_up,
    expert_down,
):
    seq_index = lax.axis_index("seq")
    seq_count = lax.axis_size("seq")
    owner_count = lax.axis_size("req")
    req_rows, tok_rows, model_width = queries.shape
    cache_rows = cache_kv.shape[2]
    held_rows = held_states.shape[1]
    local_experts = expert_gate_up.shape[0]
    expert_total = owner_count * local_experts
    my_positions = lax.dynamic_slice_in_dim(recompute_rows, seq_index * held_rows, held_rows, 1)
    projected = jnp.dot(
        held_states.reshape(req_rows * held_rows, model_width),
        key_weight,
        preferred_element_type=jnp.float32,
    )
    rotated = rotate(projected.reshape(req_rows, held_rows, KVH, HD), my_positions)
    rotated = rotated.reshape(req_rows, held_rows, KVH * HD).astype(jnp.bfloat16)
    fresh_rows = lax.all_gather(rotated, "seq", axis=1, tiled=True)
    cache_positions = seq_index * cache_rows + jnp.arange(cache_rows)
    hit_table = recompute_rows[:, None, :] == cache_positions[None, :, None]
    placed = jnp.einsum(
        "rcm,rmk->rck",
        hit_table.astype(jnp.bfloat16),
        fresh_rows,
        preferred_element_type=jnp.float32,
    ).astype(jnp.bfloat16)
    cache_keys = jnp.where(jnp.any(hit_table, axis=2)[:, :, None], placed, cache_kv[0])
    span_start = cache_spans[:, 0:1]
    span_end = cache_spans[:, 1:2]
    all_queries = lax.all_gather(queries, "seq", axis=1, tiled=True)
    step_total = all_queries.shape[1]
    cache_allowed = (cache_positions[None, :] >= span_start) & (cache_positions[None, :] < span_end)
    key_positions = seq_index * tok_rows + jnp.arange(tok_rows)
    step_allowed = key_positions[None, :] <= jnp.arange(step_total)[:, None]
    allowed = jnp.concatenate(
        [
            jnp.broadcast_to(cache_allowed[:, None, :], (req_rows, step_total, cache_rows)),
            jnp.broadcast_to(step_allowed[None], (req_rows, step_total, tok_rows)),
        ],
        axis=2,
    )
    key_rows = jnp.concatenate([cache_keys, new_kv[0]], axis=1)
    value_rows = jnp.concatenate([cache_kv[1], new_kv[1]], axis=1)
    part_out, part_log = lax.map(partial_attend, (all_queries, key_rows, value_rows, allowed))
    piece_out, piece_log = (
        lax.all_to_all(part_out[None], "seq", split_axis=2, concat_axis=0, tiled=True),
        lax.all_to_all(part_log[None], "seq", split_axis=2, concat_axis=0, tiled=True),
    )
    best_log = jnp.max(piece_log, axis=0)
    factors = jnp.exp(piece_log - best_log[None])
    factor_sum = jnp.sum(factors, axis=0)
    spread_out = piece_out.reshape(seq_count, req_rows, tok_rows, H, HD)
    combined = jnp.sum(spread_out * factors[..., None], axis=0) / factor_sum[..., None]
    attended_f = combined.reshape(req_rows, tok_rows, model_width)
    attended = attended_f.astype(jnp.bfloat16)
    attended_f = attended.astype(jnp.float32)
    mean_square = jnp.mean(attended_f * attended_f, axis=-1, keepdims=True)
    normed = (attended_f * lax.rsqrt(mean_square + 1e-06) * norm_gain).astype(jnp.bfloat16)
    route_flat = routes.reshape(req_rows, tok_rows * TOP)
    expert_match = (route_flat[:, :, None] == jnp.arange(expert_total)[None, None, :]).astype(
        jnp.int32
    )
    earlier = jnp.cumsum(expert_match, axis=1) - expert_match
    slot_index = jnp.sum(earlier * expert_match, axis=2)
    target = route_flat * CAP + slot_index
    slot_match = target[:, :, None] == jnp.arange(expert_total * CAP)[None, None, :]
    dispatch = jnp.any(
        slot_match.reshape(req_rows, tok_rows, TOP, expert_total * CAP), axis=2
    ).astype(jnp.bfloat16)
    dispatch = dispatch.reshape(req_rows, tok_rows, owner_count, local_experts, CAP)
    outgoing = jnp.einsum(
        "rtnec,rtd->nrecd", dispatch, normed, preferred_element_type=jnp.float32
    ).astype(jnp.bfloat16)
    hidden = jnp.einsum(
        "srecd,edf->srecf",
        lax.all_to_all(outgoing, "req", split_axis=0, concat_axis=0, tiled=True),
        expert_gate_up,
        preferred_element_type=jnp.float32,
    )
    active = (jax.nn.silu(hidden[..., :FF]) * hidden[..., FF:]).astype(jnp.bfloat16)
    result = jnp.einsum(
        "srecf,efd->srecd", active, expert_down, preferred_element_type=jnp.float32
    ).astype(jnp.bfloat16)
    returned = lax.all_to_all(result, "req", split_axis=0, concat_axis=0, tiled=True)
    owner_of = route_flat // local_experts
    local_of = route_flat % local_experts
    flat_index = (
        (owner_of * req_rows + jnp.arange(req_rows)[:, None]) * local_experts + local_of
    ) * CAP + slot_index
    returned_rows = jnp.take(returned.reshape(-1, model_width), flat_index.reshape(-1), axis=0)
    returned_rows = returned_rows.reshape(req_rows, tok_rows, TOP, model_width)
    mixture = jnp.einsum(
        "rtk,rtkd->rtd",
        route_weights,
        returned_rows.astype(jnp.float32),
        precision=lax.Precision.HIGHEST,
    )
    return (attended_f + mixture).astype(jnp.bfloat16)


def solution(mesh):
    in_specs = (
        P("req", "seq", None),
        P(None, "req", "seq", None),
        P(None, "req", "seq", None),
        P("req", None),
        P("req", None),
        P("req", "seq", None),
        P(),
        P(),
        P("req", "seq", None),
        P("req", "seq", None),
        P("req", None, None),
        P("req", None, None),
    )
    out_specs = P("req", "seq", None)
    return jax.shard_map(body, mesh=mesh, in_specs=in_specs, out_specs=out_specs, check_vma=False)
```

profile of v0, /device:TPU:2, one launch (start us, length us, event | category | flops | bytes accessed | tf_op | source)
XLA Modules:
  0.0 298.9 jit_solution(2745684699913608374)
XLA Ops:
  6.5 1.8 copy.65
  9.2 1.7 copy.63
  13.4 10.8 %all_gather.6 = bf16[2,256,512]{2,1,0:T(8,128)(2,1)S(1)} all-gather(bf16[2,32,512]{2,1,0:T(8,128)(2,1)S(1)} %convert_element_type.67), channel_id=1, replica_groups=mesh['seq'=8,'req'=4] {'seq'}, dimensions={1}, use_global_device_ids=true | all-gather | bytes 589824 | tf_op jit(solution)/shard_map/all_gather | solution.py:89
  25.2 0.9 pad_maximum_fusion.1
  26.1 1.0 pad_maximum_fusion
  27.1 10.3 %all-gather.2.cloned.1.call-done = bf16[2,256,1536]{2,0,1:T(2,128)(2,1)} async-done(((bf16[2,32,1536]{2,0,1:T(2,128)(2,1)}), bf16[2,256,1536]{2,0,1:T(2,128)(2,1)}) %all-gather.2.cloned.1.call-update) | async-done | bytes 1572880 | tf_op jit(solution)/shard_map/all_gather | solution.py:101
  37.4 4.9 %copy.67 = bf16[2,256,1536]{1,2,0:T(8,128)(2,1)} copy(bf16[2,256,1536]{2,0,1:T(2,128)(2,1)} %all-gather.2.cloned.1.call-done) | data formatting | bytes 3145728 | tf_op jit(solution)/shard_map/while | solution.py:115
  42.3 78.1 %while.12 = (s32[]{:T(128)}, f32[2,256,1536]{2,0,1:T(2,128)}, f32[2,256,24]{1,2,0:T(8,128)S(1)}, bf16[2,288,512]{1,2,0:T(8,128)(2,1)}, pred[2,256,288]{1,2,0:T(8...) while((s32[]{:T(128)}, f32[2,256,1536]{2,0,1:T(2,128)}, ...), condition=%wide.region_4.5_spmd, body=%wide.region_1.4_spmd.sunk | while | flops 472836096 | bytes 62791824 | solution.py:115
  42.3 1.2 constant_dynamic-slice_fusion.8
  43.5 1.0 constant_dynamic-slice_fusion.7
  44.7 1.2 fusion.81
  45.9 1.5 fusion.82
  47.4 1.4 copy-done.2
  48.8 1.0 constant_dynamic-slice_fusion.6
  49.9 4.8 %bitcast_divide_fusion.2 = f32[256,8,3,64]{0,3,2,1:T(8,128)S(1)} fusion(bf16[288,8,64,1]{0,2,3,1:T(8,128)(2,1)S(1)} %bitcast.165, f32[8,288,256,3]{2,1,3,0:T(8,128)} %copy-done.2, f32[8,3,256]{2,1,0:T(4,128)S(1)} %get-tuple-element.152, pred[256,288]{0,1:T(8,128)(4,1)S(1)} %dynamic-slice_bitcast_fusion.2, f32[256,8,3]{0,2,1:T(4,128)S(1)} %bitcast.167), kind=kOutput, calls=%fused_computation.8.clone.1 | convolution fusion | flops 233963520 | bytes 9068544 | tf_op jit(solution)/shard_map/while/body/eval_jaxpr/kgqn,nkd->qkgd/dot_general | solution.py:50
  54.7 1.2 copy.114
  55.9 25.4 %dynamic_update_slice.12 = f32[2,256,1536]{2,0,1:T(2,128)} dynamic-update-slice(f32[2,256,1536]{2,0,1:T(2,128)} %get-tuple-element.163, f32[1,256,1536]{2,0,1:T(1,128)S(1)} %copy.114, s32[]{:T(128)} %get-tuple-element.162, s32[]{:T(128)} %constant.54.clone.1..sunk, s32[]{:T(128)} %constant.54.clone.1..sunk) | dynamic-update-slice | bytes 3145732 | tf_op jit(solution)/shard_map/while/body/jit(dynamic_update_index_in_dim)/dynamic_update_slice | solution.py:115
  81.3 1.2 constant_dynamic-slice_fusion.8
  82.5 1.0 constant_dynamic-slice_fusion.7
  83.7 1.2 fusion.81
  84.9 1.5 fusion.82
  86.4 1.4 copy-done.2
  87.9 1.0 constant_dynamic-slice_fusion.6
  88.9 4.8 %bitcast_divide_fusion.2 = f32[256,8,3,64]{0,3,2,1:T(8,128)S(1)} fusion(bf16[288,8,64,1]{0,2,3,1:T(8,128)(2,1)S(1)} %bitcast.165, f32[8,288,256,3]{2,1,3,0:T(8,128)} %copy-done.2, f32[8,3,256]{2,1,0:T(4,128)S(1)} %get-tuple-element.152, pred[256,288]{0,1:T(8,128)(4,1)S(1)} %dynamic-slice_bitcast_fusion.2, f32[256,8,3]{0,2,1:T(4,128)S(1)} %bitcast.167), kind=kOutput, calls=%fused_computation.8.clone.1 | convolution fusion | flops 233963520 | bytes 9068544 | tf_op jit(solution)/shard_map/while/body/eval_jaxpr/kgqn,nkd->qkgd/dot_general | solution.py:50
  93.7 1.2 copy.114
  94.9 25.4 %dynamic_update_slice.12 = f32[2,256,1536]{2,0,1:T(2,128)} dynamic-update-slice(f32[2,256,1536]{2,0,1:T(2,128)} %get-tuple-element.163, f32[1,256,1536]{2,0,1:T(1,128)S(1)} %copy.114, s32[]{:T(128)} %get-tuple-element.162, s32[]{:T(128)} %constant.54.clone.1..sunk, s32[]{:T(128)} %constant.54.clone.1..sunk) | dynamic-update-slice | bytes 3145732 | tf_op jit(solution)/shard_map/while/body/jit(dynamic_update_index_in_dim)/dynamic_update_slice | solution.py:115
  120.9 6.6 %all_to_all.43 = f32[8,1,1536]{2,1,0:T(1,128)S(1)} all-to-all(f32[8,1,1536]{2,1,0:T(1,128)S(1)} %reshape.329), channel_id=1, replica_groups=mesh['seq'=8,'req'=4] {'seq'}, dimensions={0} | all-to-all | bytes 98304 | tf_op jit(solution)/shard_map/all_to_all | solution.py:118
  127.5 5.2 %all-to-all-start = ((f32[1,2,256,1536]{3,1,0,2:T(2,128)}), f32[1,2,256,1536]{3,1,0,2:T(2,128)S(1)}, u32[]{:S(2)}, u32[]{:S(2)}) async-start(f32[1,2,256,1536]{3,1,0,2:T(2,128)} %bitcast.168), calls=%async_computation | async-start | bytes 6291456 | tf_op jit(solution)/shard_map/all_to_all | solution.py:117
  132.9 1.2 reduce-window.6
  136.5 1.2 reshape.330
  137.7 1.1 copy.71
  138.9 1.3 fusion.63
  140.2 1.8 copy.72
  142.0 4.9 %mul.189 = f32[8,2,32,24,64]{4,3,2,0,1:T(8,128)} broadcast(f32[8,2,32,24]{3,2,0,1:T(8,128)} %copy.72), dimensions={0,1,2,3} | broadcast | bytes 3194880 | tf_op jit(solution)/shard_map/mul | solution.py:124
  146.9 6.2 %mul.190 = f32[8,1,2,32,1536]{4,3,0,2,1:T(8,128)} reshape(f32[8,2,32,24,64]{4,3,2,0,1:T(8,128)} %mul.189) | data formatting | bytes 6291456 | tf_op jit(solution)/shard_map/mul | solution.py:124
  153.2 1.2 div.53
  154.3 2.1 div.54
  156.4 12.6 %all-to-all-done = f32[1,2,256,1536]{3,1,0,2:T(2,128)S(1)} async-done(((f32[1,2,256,1536]{3,1,0,2:T(2,128)}), f32[1,2,256,1536]{3,1,0,2:T(2,128)S(1)}, u32[]{:S(2)}, u32[]{:S(2)}) %all-to-all-start) | async-done | bytes 3145760 | tf_op jit(solution)/shard_map/all_to_all | solution.py:117
  169.7 1.3 copy-done.3
  173.0 50.3 %all_to_all.44 = bf16[4,2,5,16,1536]{4,3,1,2,0:T(8,128)(2,1)S(1)} all-to-all(bf16[4,2,5,16,1536]{4,3,1,2,0:T(8,128)(2,1)S(1)} %copy.83), channel_id=1, replica_groups=mesh['seq'=8,'req'=4] {'req'}, dimensions={0} | all-to-all | bytes 3932160 | tf_op jit(solution)/shard_map/all_to_all | solution.py:147
  223.3 8.1 %fusion.22 = f32[4,2,5,16,1024]{4,3,1,0,2:T(8,128)S(1)} fusion(bf16[5,1536,1024]{2,1,0:T(8,128)(2,1)} %param.24, bf16[4,2,5,16,1536]{4,3,1,2,0:T(8,128)(2,1)S(1)} %all_to_all.44), kind=kOutput, calls=%fused_computation.27 | convolution fusion | flops 2013265920 | bytes 20316160 | tf_op jit(solution)/shard_map/srecd,edf->srecf/dot_general | solution.py:145
  231.4 1.4 fusion.18
  232.8 1.4 copy.85
  234.2 4.5 %all-to-all-start.3 = ((bf16[4,2,5,16,1536]{4,3,1,2,0:T(8,128)(2,1)}), bf16[4,2,5,16,1536]{4,3,1,2,0:T(8,128)(2,1)}, u32[]{:S(2)}, u32[]{:S(2)}) async-start(bf16[4,2,5,16,1536]{4,3,1,2,0:T(8,128)(2,1)} %copy.85), calls=%async_computation.3 | async-start | bytes 3932160 | tf_op jit(solution)/shard_map/all_to_all | solution.py:155
  239.3 44.5 %all-to-all-done.3 = bf16[4,2,5,16,1536]{4,3,1,2,0:T(8,128)(2,1)} async-done(((bf16[4,2,5,16,1536]{4,3,1,2,0:T(8,128)(2,1)}), bf16[4,2,5,16,1536]{4,3,1,2,0:T(8,128)(2,1)}, u32[]{:S(2)}, u32[]{:S(2)}) %all-to-all-start.3) | async-done | bytes 1966112 | tf_op jit(solution)/shard_map/all_to_all | solution.py:155
  283.8 1.7 copy.86
  285.5 3.0 gather_fusion
  288.4 2.9 fusion.27
  (110 shorter events, 11.8 us)
Async XLA Ops:
  6.5 4.6 %copy-start = (bf16[2,32,1536]{2,1,0:T(8,128)(2,1)S(1)}, bf16[2,32,1536]{2,1,0:T(8,128)(2,1)}, u32[]{:S(2)}) copy-start(bf16[2,32,1536]{2,1,0:T(8,128)(2,1)} %param.19) | copy-start | bytes 589828
  6.5 30.8 %all-gather.2.cloned.1.call-start = ((), (), s32[]{:S(2)}) async-start(), calls=%async_computation.4 | async-start | bytes 1769472 | tf_op jit(solution)/shard_map/all_gather | solution.py:101
  10.9 1.6 copy-start.6
  12.0 1.0 slice-start
  12.1 1.1 copy-start.14
  12.3 12.3 %copy-start.13 = (s32[2,256]{1,0:T(2,128)S(1)}, s32[2,256]{1,0:T(2,128)}, u32[]{:S(2)}) copy-start(s32[2,256]{1,0:T(2,128)} %param.18) | copy-start | bytes 6148
  12.4 12.5 %copy-start.4 = (bf16[2,2,256,512]{3,2,1,0:T(8,128)(2,1)S(1)}, bf16[2,2,256,512]{3,2,1,0:T(8,128)(2,1)}, u32[]{:S(2)}) copy-start(bf16[2,2,256,512]{3,2,1,0:T(8,128)(2,1)} %param.16) | copy-start | bytes 3145732
  45.9 2.9 copy-start.2
  84.9 2.9 copy-start.2
  127.5 5.2 %copy-start.11 = (s32[2,32,8]{1,2,0:T(8,128)S(1)}, s32[2,32,8]{1,2,0:T(8,128)}, u32[]{:S(2)}) copy-start(s32[2,32,8]{1,2,0:T(8,128)} %param.22) | copy-start | bytes 6148
  127.5 41.5 %all-to-all-start = ((f32[1,2,256,1536]{3,1,0,2:T(2,128)}), f32[1,2,256,1536]{3,1,0,2:T(2,128)S(1)}, u32[]{:S(2)}, u32[]{:S(2)}) async-start(f32[1,2,256,1536]{3,1,0,2:T(2,128)} %bitcast.168), calls=%async_computation | async-start | bytes 6291456 | tf_op jit(solution)/shard_map/all_to_all | solution.py:117
  134.6 0.7 copy-start.8
  146.9 6.2 %copy-start.7 = (f32[2,32,24]{1,2,0:T(8,128)S(1)}, f32[2,32,24]{1,2,0:T(8,128)}, u32[]{:S(2)}) copy-start(f32[2,32,24]{1,2,0:T(8,128)} %get-tuple-element.93) | copy-start | bytes 18436
  169.0 1.9 copy-start.3
  170.9 1.0 copy-start.5
  170.9 1.1 copy-start.10
  173.0 58.4 %slice-start.1 = ((s8[7864320]{0:T(1024)(128)(4,1)}), s8[4194304]{0:T(1024)(128)(4,1)S(1)}, s32[]{:S(2)}) async-start(s8[7864320]{0:T(1024)(128)(4,1)} %bitcast.179), calls=%async_computation.6 | async-start | bytes 8388608
  223.3 8.1 %slice-start.2 = ((s8[7864320]{0:T(1024)(128)(4,1)}), s8[3670016]{0:T(1024)(128)(4,1)S(1)}, s32[]{:S(2)}) async-start(s8[7864320]{0:T(1024)(128)(4,1)} %bitcast.179), calls=%async_computation.7 | async-start | bytes 7340032
  234.2 4.9 %copy-start.9 = (s32[2,256]{1,0:T(2,128)S(1)}, s32[2,256]{1,0:T(2,128)}, u32[]{:S(2)}) copy-start(s32[2,256]{1,0:T(2,128)} %copy-done.8) | copy-start | bytes 6148
  234.2 4.9 %copy-start.12 = (f32[2,32,8]{1,2,0:T(8,128)S(1)}, f32[2,32,8]{1,2,0:T(8,128)}, u32[]{:S(2)}) copy-start(f32[2,32,8]{1,2,0:T(8,128)} %param.23) | copy-start | bytes 6148
  234.2 49.5 %all-to-all-start.3 = ((bf16[4,2,5,16,1536]{4,3,1,2,0:T(8,128)(2,1)}), bf16[4,2,5,16,1536]{4,3,1,2,0:T(8,128)(2,1)}, u32[]{:S(2)}, u32[]{:S(2)}) async-start(bf16[4,2,5,16,1536]{4,3,1,2,0:T(8,128)(2,1)} %copy.85), calls=%async_computation.3 | async-start | bytes 3932160 | tf_op jit(solution)/shard_map/all_to_all | solution.py:155
  285.4 6.6 %copy-start.1 = (bf16[2,32,1536]{2,1,0:T(8,128)(2,1)S(1)}, bf16[2,32,1536]{2,1,0:T(8,128)(2,1)}, u32[]{:S(2)}) copy-start(bf16[2,32,1536]{2,1,0:T(8,128)(2,1)} %param.19) | copy-start | bytes 589828
Sparse Core Ops, SparseCore 0:
  9.2 28.0 all-gather.1
where the time goes:
time: 303 us; the launch traced here: 299 us
  local copies, waits for them, and re-layouts  102 us (34%)
  blocking collectives  67.7 us (22%)
  waiting for transfers between devices  67.4 us (22%)
  matrix products  26.3 us (9%)
  between operations  13.9 us (5%)
  other arithmetic  12 us (4%)
  starting transfers between devices  9.69 us (3%)
    dynamic_update_slice x6, local copies, waits for them, and re-layouts, body(): lax.map(partial_attend, (all_queries, key_rows, value_rows, allowed))  53.2 us
    all_to_all x1, blocking collectives, body(): lax.all_to_all(outgoing, 'req', split_axis=0, concat_axis=0, tiled=True)  50.3 us
    all_to_all x1, waiting for transfers between devices, body(): lax.all_to_all(result, 'req', split_axis=0, concat_axis=0, tiled=True)  44.5 us
    all_to_all x1, waiting for transfers between devices, body(): lax.all_to_all(part_out[None], 'seq', split_axis=2, concat_axis=0, tiled=...  12.6 us
    mul x2, local copies, waits for them, and re-layouts, body(): spread_out * factors[..., None]  11.1 us
    all_gather x1, blocking collectives, body(): fresh_rows = lax.all_gather(rotated, 'seq', axis=1, tiled=True)  10.8 us
    all_gather x1, waiting for transfers between devices, body(): all_queries = lax.all_gather(queries, 'seq', axis=1, tiled=True)  10.3 us
    dot_general x2, matrix products, partial_attend(): jnp.einsum('kgqn,nkd->qkgd', weights, value_heads, preferred_element_type...  9.64 us
  transfers between devices with their start and end apart: 3, of which 3 were waited for; matrix products, arithmetic and copies ran while one was open for 11% of the time, Pallas kernels for 0%

commit v1 on v0

--- a/solution.py
+++ b/solution.py
@@ -11,6 +11,38 @@
 CAP = 16
 NEG = -1e30
 THETA = 10000.0
+
+
+def keep_up_indices(piece_in, which_dim, page):
+    finding = piece_in.shape
+    current_value = piece_in.reshape(
+        *finding[:which_dim], page, finding[which_dim] // page, *finding[which_dim + 1 :]
+    )
+    vec_out = jnp.moveaxis(current_value, which_dim, 0)
+    return vec_out
+
+
+def store_the_edges(point, d0):
+    point = jnp.moveaxis(point, 0, d0)
+    v1 = point.shape
+    passed = point.reshape(*v1[:d0], v1[d0] * v1[d0 + 1], *v1[d0 + 2 :])
+    return passed
+
+
+def _group_vectors(inner_x, net_axis, sample, u):
+    tile_out, b_now = (jax.lax.axis_size(net_axis), jax.lax.axis_index(net_axis))
+    formed = keep_up_indices(inner_x, sample, tile_out)
+    history = [formed[b_now]]
+    j0 = 1
+    while j0 < tile_out:
+        known = formed[b_now ^ j0]
+        history.append(
+            jax.lax.ppermute(known, net_axis, [(idx, idx ^ j0) for idx in range(tile_out)])
+        )
+        j0 += 1
+    formed = jnp.stack(history, axis=0)[b_now ^ jnp.arange(tile_out)]
+    response = store_the_edges(formed, u)
+    return response
 
 
 def rotate(key_heads, positions):
@@ -152,7 +184,7 @@
     result = jnp.einsum(
         "srecf,efd->srecd", active, expert_down, preferred_element_type=jnp.float32
     ).astype(jnp.bfloat16)
-    returned = lax.all_to_all(result, "req", split_axis=0, concat_axis=0, tiled=True)
+    returned = _group_vectors(result, "req", 0, 0)
     owner_of = route_flat // local_experts
     local_of = route_flat % local_experts
     flat_index = (

time: 303 us -> 304 us (level)
  the two profiles are of different devices: /device:TPU:2 before, /device:TPU:10 now
where the time goes in v1:
time: 304 us; the launch traced here: 300 us
  waiting for transfers between devices  107 us (35%)
  local copies, waits for them, and re-layouts  104 us (34%)
  matrix products  29.2 us (10%)
  blocking collectives  17.4 us (6%)
  starting transfers between devices  15.2 us (5%)
  between operations  13.9 us (5%)
  other arithmetic  13.5 us (4%)
    dynamic_update_slice x6, local copies, waits for them, and re-layouts, body(): lax.map(partial_attend, (all_queries, key_rows, value_rows, allowed))  53.2 us
    all_to_all x1, waiting for transfers between devices, body(): lax.all_to_all(outgoing, 'req', split_axis=0, concat_axis=0, tiled=True)  42.3 us
    ppermute x3, waiting for transfers between devices, _group_vectors(): jax.lax.ppermute(known, net_axis, [(idx, idx ^ j0) for idx in range(tile_...  41.5 us
    all_to_all x1, waiting for transfers between devices, body(): lax.all_to_all(part_out[None], 'seq', split_axis=2, concat_axis=0, tiled=...  12.6 us
    mul x2, local copies, waits for them, and re-layouts, body(): spread_out * factors[..., None]  11.1 us
    all_gather x1, blocking collectives, body(): fresh_rows = lax.all_gather(rotated, 'seq', axis=1, tiled=True)  10.8 us
    all_gather x1, waiting for transfers between devices, body(): all_queries = lax.all_gather(queries, 'seq', axis=1, tiled=True)  10.2 us
    dot_general x2, matrix products, partial_attend(): jnp.einsum('kgqn,nkd->qkgd', weights, value_heads, preferred_element_type...  9.64 us
  transfers between devices with their start and end apart: 6, of which 6 were waited for; matrix products, arithmetic and copies ran while one was open for 10% of the time, Pallas kernels for 0%

profile of v1, /device:TPU:10, one launch (start us, length us, event | category | flops | bytes accessed | tf_op | source)
XLA Modules:
  0.0 299.6 jit_solution(16553558773765664176)
XLA Ops:
  6.5 1.8 copy.73
  9.2 1.7 copy.71
  13.5 10.8 %all_gather.6 = bf16[2,256,512]{2,1,0:T(8,128)(2,1)S(1)} all-gather(bf16[2,32,512]{2,1,0:T(8,128)(2,1)S(1)} %convert_element_type.65), channel_id=1, replica_groups=mesh['seq'=8,'req'=4] {'seq'}, dimensions={1}, use_global_device_ids=true | all-gather | bytes 589824 | tf_op jit(solution)/shard_map/all_gather | solution.py:121
  27.0 10.2 %all-gather.2.cloned.1.call-done = bf16[2,256,1536]{2,0,1:T(2,128)(2,1)} async-done(((bf16[2,32,1536]{2,0,1:T(2,128)(2,1)}), bf16[2,256,1536]{2,0,1:T(2,128)(2,1)}) %all-gather.2.cloned.1.call-update) | async-done | bytes 1572880 | tf_op jit(solution)/shard_map/all_gather | solution.py:133
  37.3 4.9 %copy.75 = bf16[2,256,1536]{1,2,0:T(8,128)(2,1)} copy(bf16[2,256,1536]{2,0,1:T(2,128)(2,1)} %all-gather.2.cloned.1.call-done) | data formatting | bytes 3145728 | tf_op jit(solution)/shard_map/while | solution.py:147
  42.2 78.1 %while.12 = (s32[]{:T(128)}, f32[2,256,1536]{2,0,1:T(2,128)}, f32[2,256,24]{1,2,0:T(8,128)S(1)}, bf16[2,288,512]{1,2,0:T(8,128)(2,1)}, pred[2,256,288]{1,2,0:T(8...) while((s32[]{:T(128)}, f32[2,256,1536]{2,0,1:T(2,128)}, ...), condition=%wide.region_4.5_spmd, body=%wide.region_1.4_spmd.sunk | while | flops 472836096 | bytes 62791824 | solution.py:147
  42.2 1.2 constant_dynamic-slice_fusion.9
  44.6 1.2 fusion.80
  45.8 1.5 fusion.81
  47.3 1.4 copy-done.2
  49.8 4.8 %bitcast_divide_fusion.2 = f32[256,8,3,64]{0,3,2,1:T(8,128)S(1)} fusion(bf16[288,8,64,1]{0,2,3,1:T(8,128)(2,1)S(1)} %bitcast.184, f32[8,288,256,3]{2,1,3,0:T(8,128)} %copy-done.2, f32[8,3,256]{2,1,0:T(4,128)S(1)} %get-tuple-element.156, pred[256,288]{0,1:T(8,128)(4,1)S(1)} %dynamic-slice_bitcast_fusion.6, f32[256,8,3]{0,2,1:T(4,128)S(1)} %bitcast.186), kind=kOutput, calls=%fused_computation.9.clone.1 | convolution fusion | flops 233963520 | bytes 9068544 | tf_op jit(solution)/shard_map/while/body/eval_jaxpr/kgqn,nkd->qkgd/dot_general | solution.py:82
  54.6 1.2 copy.127
  55.8 25.4 %dynamic_update_slice.12 = f32[2,256,1536]{2,0,1:T(2,128)} dynamic-update-slice(f32[2,256,1536]{2,0,1:T(2,128)} %get-tuple-element.167, f32[1,256,1536]{2,0,1:T(1,128)S(1)} %copy.127, s32[]{:T(128)} %get-tuple-element.166, s32[]{:T(128)} %constant.49.clone.1..sunk, s32[]{:T(128)} %constant.49.clone.1..sunk) | dynamic-update-slice | bytes 3145732 | tf_op jit(solution)/shard_map/while/body/jit(dynamic_update_index_in_dim)/dynamic_update_slice | solution.py:147
  81.2 1.2 constant_dynamic-slice_fusion.9
  83.6 1.2 fusion.80
  84.8 1.5 fusion.81
  86.3 1.4 copy-done.2
  88.8 4.8 %bitcast_divide_fusion.2 = f32[256,8,3,64]{0,3,2,1:T(8,128)S(1)} fusion(bf16[288,8,64,1]{0,2,3,1:T(8,128)(2,1)S(1)} %bitcast.184, f32[8,288,256,3]{2,1,3,0:T(8,128)} %copy-done.2, f32[8,3,256]{2,1,0:T(4,128)S(1)} %get-tuple-element.156, pred[256,288]{0,1:T(8,128)(4,1)S(1)} %dynamic-slice_bitcast_fusion.6, f32[256,8,3]{0,2,1:T(4,128)S(1)} %bitcast.186), kind=kOutput, calls=%fused_computation.9.clone.1 | convolution fusion | flops 233963520 | bytes 9068544 | tf_op jit(solution)/shard_map/while/body/eval_jaxpr/kgqn,nkd->qkgd/dot_general | solution.py:82
  93.6 1.2 copy.127
  94.8 25.4 %dynamic_update_slice.12 = f32[2,256,1536]{2,0,1:T(2,128)} dynamic-update-slice(f32[2,256,1536]{2,0,1:T(2,128)} %get-tuple-element.167, f32[1,256,1536]{2,0,1:T(1,128)S(1)} %copy.127, s32[]{:T(128)} %get-tuple-element.166, s32[]{:T(128)} %constant.49.clone.1..sunk, s32[]{:T(128)} %constant.49.clone.1..sunk) | dynamic-update-slice | bytes 3145732 | tf_op jit(solution)/shard_map/while/body/jit(dynamic_update_index_in_dim)/dynamic_update_slice | solution.py:147
  120.8 6.6 %all_to_all.38 = f32[8,1,1536]{2,1,0:T(1,128)S(1)} all-to-all(f32[8,1,1536]{2,1,0:T(1,128)S(1)} %reshape.360), channel_id=1, replica_groups=mesh['seq'=8,'req'=4] {'seq'}, dimensions={0} | all-to-all | bytes 98304 | tf_op jit(solution)/shard_map/all_to_all | solution.py:150
  127.4 5.2 %all-to-all-start = ((f32[1,2,256,1536]{3,1,0,2:T(2,128)}), f32[1,2,256,1536]{3,1,0,2:T(2,128)S(1)}, u32[]{:S(2)}, u32[]{:S(2)}) async-start(f32[1,2,256,1536]{3,1,0,2:T(2,128)} %bitcast.187), calls=%async_computation | async-start | bytes 6291456 | tf_op jit(solution)/shard_map/all_to_all | solution.py:149
  132.9 1.2 reduce-window.6
  136.5 1.2 reshape.361
  137.6 1.1 copy.79
  138.8 1.3 fusion.62
  140.1 1.8 copy.80
  141.9 4.9 %mul.189 = f32[8,2,32,24,64]{4,3,2,0,1:T(8,128)} broadcast(f32[8,2,32,24]{3,2,0,1:T(8,128)} %copy.80), dimensions={0,1,2,3} | broadcast | bytes 3194880 | tf_op jit(solution)/shard_map/mul | solution.py:156
  146.8 6.2 %mul.190 = f32[8,1,2,32,1536]{4,3,0,2,1:T(8,128)} reshape(f32[8,2,32,24,64]{4,3,2,0,1:T(8,128)} %mul.189) | data formatting | bytes 6291456 | tf_op jit(solution)/shard_map/mul | solution.py:156
  153.1 1.2 div.53
  154.2 2.1 div.54
  156.4 12.6 %all-to-all-done = f32[1,2,256,1536]{3,1,0,2:T(2,128)S(1)} async-done(((f32[1,2,256,1536]{3,1,0,2:T(2,128)}), f32[1,2,256,1536]{3,1,0,2:T(2,128)S(1)}, u32[]{:S(2)}, u32[]{:S(2)}) %all-to-all-start) | async-done | bytes 3145760 | tf_op jit(solution)/shard_map/all_to_all | solution.py:149
  169.6 1.3 copy-done.3
  172.7 1.5 copy.91
  174.2 5.1 %all-to-all-start.2 = ((bf16[4,2,5,16,1536]{4,3,1,2,0:T(8,128)(2,1)}), bf16[4,2,5,16,1536]{4,3,1,2,0:T(8,128)(2,1)S(1)}, u32[]{:S(2)}, u32[]{:S(2)}) async-start(bf16[4,2,5,16,1536]{4,3,1,2,0:T(8,128)(2,1)} %copy.91), calls=%async_computation.2 | async-start | bytes 3932160 | tf_op jit(solution)/shard_map/all_to_all | solution.py:179
  179.4 42.3 %all-to-all-done.2 = bf16[4,2,5,16,1536]{4,3,1,2,0:T(8,128)(2,1)S(1)} async-done(((bf16[4,2,5,16,1536]{4,3,1,2,0:T(8,128)(2,1)}), bf16[4,2,5,16,1536]{4,3,1,2,0:T(8,128)(2,1)S(1)}, u32[]{:S(2)}, u32[]{:S(2)}) %all-to-all-start.2) | async-done | bytes 1966112 | tf_op jit(solution)/shard_map/all_to_all | solution.py:179
  221.7 7.7 %fusion.19 = f32[4,2,5,16,1024]{4,3,1,0,2:T(8,128)S(1)} fusion(bf16[5,1536,1024]{2,1,0:T(8,128)(2,1)} %param.24, bf16[4,2,5,16,1536]{4,3,1,2,0:T(8,128)(2,1)S(1)} %all-to-all-done.2), kind=kOutput, calls=%fused_computation.28 | convolution fusion | flops 2013265920 | bytes 20316160 | tf_op jit(solution)/shard_map/srecd,edf->srecf/dot_general | solution.py:177
  229.4 4.7 %fusion.14 = bf16[5,4,2,16,1536]{4,3,2,1,0:T(8,128)(2,1)S(1)} fusion(bf16[5,512,1536]{2,1,0:T(8,128)(2,1)} %param.25, f32[4,2,5,16,1024]{4,3,1,0,2:T(8,128)S(1)} %fusion.19), kind=kOutput, calls=%fused_computation.22 | convolution fusion | flops 1009582080 | bytes 12451840 | tf_op jit(solution)/shard_map/srecf,efd->srecd/dot_general | solution.py:184
  234.3 3.3 %collective-permute-start = (bf16[1,2,5,16,1536]{4,3,1,2,0:T(8,128)(2,1)S(1)}, bf16[1,2,5,16,1536]{4,3,1,2,0:T(8,128)(2,1)S(1)}, u32[]{:S(2)}, u32[]{:S(2)}) collective-permute-start(bf16[1,2,5,16,1536]{4,3,1,2,0:T(8,128)(2,1)S(1)} %get-tuple-element.98), channel_id=1, source_target_pairs={{0,1},{1,0},{2,3},{3,2},{4,5},{5,4},{6,7},{7,6},{8,9},{9,8},{10,11... | collective-permute-start | bytes 1474568 | tf_op jit(solution)/shard_map/ppermute | solution.py:40
  237.7 1.5 collective-permute-start.2
  239.6 17.0 %collective-permute-done = bf16[1,2,5,16,1536]{4,3,1,2,0:T(8,128)(2,1)S(1)} collective-permute-done((bf16[1,2,5,16,1536]{4,3,1,2,0:T(8,128)(2,1)S(1)}, bf16[1,2,5,16,1536]{4,3,1,2,0:T(8,128)(2,1)S(1)}, u32[]{:S(2)}, u32[]{:S(2)}) %collective-permute-start) | collective-permute-done | bytes 491552 | tf_op jit(solution)/shard_map/ppermute | solution.py:40
  256.7 13.8 %collective-permute-done.1 = bf16[1,2,5,16,1536]{4,3,1,2,0:T(8,128)(2,1)S(1)} collective-permute-done((bf16[1,2,5,16,1536]{4,3,1,2,0:T(8,128)(2,1)S(1)}, bf16[1,2,5,16,1536]{4,3,1,2,0:T(8,128)(2,1)S(1)}, u32[]{:S(2)}, u32[]{:S(2)}) %collective-permute-start.1) | collective-permute-done | bytes 491552 | tf_op jit(solution)/shard_map/ppermute | solution.py:40
  270.4 10.7 %collective-permute-done.2 = bf16[1,2,5,16,1536]{4,3,1,0,2:T(8,128)(2,1)} collective-permute-done((bf16[1,2,5,16,1536]{4,3,1,0,2:T(8,128)(2,1)S(1)}, bf16[1,2,5,16,1536]{4,3,1,0,2:T(8,128)(2,1)}, u32[]{:S(2)}, u32[]{:S(2)}) %collective-permute-start.2) | collective-permute-done | bytes 491552 | tf_op jit(solution)/shard_map/ppermute | solution.py:40
  281.1 1.4 maximum_bitcast_fusion
  282.5 2.0 gather_fusion
  284.5 1.7 copy.96
  286.2 3.0 gather_fusion.1
  289.2 2.9 fusion.24
  (116 shorter events, 17.8 us)
Async XLA Ops:
  6.5 4.6 %copy-start = (bf16[2,32,1536]{2,1,0:T(8,128)(2,1)S(1)}, bf16[2,32,1536]{2,1,0:T(8,128)(2,1)}, u32[]{:S(2)}) copy-start(bf16[2,32,1536]{2,1,0:T(8,128)(2,1)} %param.19) | copy-start | bytes 589828
  6.5 30.7 %all-gather.2.cloned.1.call-start = ((), (), s32[]{:S(2)}) async-start(), calls=%async_computation.3 | async-start | bytes 1769472 | tf_op jit(solution)/shard_map/all_gather | solution.py:133
  10.9 1.6 copy-start.7
  12.0 1.0 slice-start
  12.1 1.1 copy-start.15
  12.3 12.2 %copy-start.14 = (s32[2,256]{1,0:T(2,128)S(1)}, s32[2,256]{1,0:T(2,128)}, u32[]{:S(2)}) copy-start(s32[2,256]{1,0:T(2,128)} %param.18) | copy-start | bytes 6148
  12.4 12.4 %copy-start.4 = (bf16[2,2,256,512]{3,2,1,0:T(8,128)(2,1)S(1)}, bf16[2,2,256,512]{3,2,1,0:T(8,128)(2,1)}, u32[]{:S(2)}) copy-start(bf16[2,2,256,512]{3,2,1,0:T(8,128)(2,1)} %param.16) | copy-start | bytes 3145732
  45.8 2.9 copy-start.2
  84.8 2.9 copy-start.2
  127.4 5.2 %copy-start.12 = (s32[2,32,8]{1,2,0:T(8,128)S(1)}, s32[2,32,8]{1,2,0:T(8,128)}, u32[]{:S(2)}) copy-start(s32[2,32,8]{1,2,0:T(8,128)} %param.22) | copy-start | bytes 6148
  127.4 41.5 %all-to-all-start = ((f32[1,2,256,1536]{3,1,0,2:T(2,128)}), f32[1,2,256,1536]{3,1,0,2:T(2,128)S(1)}, u32[]{:S(2)}, u32[]{:S(2)}) async-start(f32[1,2,256,1536]{3,1,0,2:T(2,128)} %bitcast.187), calls=%async_computation | async-start | bytes 6291456 | tf_op jit(solution)/shard_map/all_to_all | solution.py:149
  134.5 0.7 copy-start.9
  146.8 6.2 %copy-start.8 = (f32[2,32,24]{1,2,0:T(8,128)S(1)}, f32[2,32,24]{1,2,0:T(8,128)}, u32[]{:S(2)}) copy-start(f32[2,32,24]{1,2,0:T(8,128)} %get-tuple-element.93) | copy-start | bytes 18436
  169.0 1.9 copy-start.3
  170.8 1.0 copy-start.5
  170.8 1.1 copy-start.11
  174.2 47.5 %all-to-all-start.2 = ((bf16[4,2,5,16,1536]{4,3,1,2,0:T(8,128)(2,1)}), bf16[4,2,5,16,1536]{4,3,1,2,0:T(8,128)(2,1)S(1)}, u32[]{:S(2)}, u32[]{:S(2)}) async-start(bf16[4,2,5,16,1536]{4,3,1,2,0:T(8,128)(2,1)} %copy.91), calls=%async_computation.2 | async-start | bytes 3932160 | tf_op jit(solution)/shard_map/all_to_all | solution.py:179
  234.1 5.3 %copy-start.10 = (s32[2,256]{1,0:T(2,128)S(1)}, s32[2,256]{1,0:T(2,128)}, u32[]{:S(2)}) copy-start(s32[2,256]{1,0:T(2,128)} %copy-done.9) | copy-start | bytes 6148
  234.1 5.4 %copy-start.13 = (f32[2,32,8]{1,2,0:T(8,128)S(1)}, f32[2,32,8]{1,2,0:T(8,128)}, u32[]{:S(2)}) copy-start(f32[2,32,8]{1,2,0:T(8,128)} %param.23) | copy-start | bytes 6148
  234.3 22.4 %collective-permute-start = (bf16[1,2,5,16,1536]{4,3,1,2,0:T(8,128)(2,1)S(1)}, bf16[1,2,5,16,1536]{4,3,1,2,0:T(8,128)(2,1)S(1)}, u32[]{:S(2)}, u32[]{:S(2)}) collective-permute-start(bf16[1,2,5,16,1536]{4,3,1,2,0:T(8,128)(2,1)S(1)} %get-tuple-element.98), channel_id=1, source_target_pairs={{0,1},{1,0},{2,3},{3,2},{4,5},{5,4},{6,7},{7,6},{8,9},{9,8},{10,11... | collective-permute-start | bytes 1474568 | tf_op jit(solution)/shard_map/ppermute | solution.py:40
  237.6 32.8 %collective-permute-start.1 = (bf16[1,2,5,16,1536]{4,3,1,2,0:T(8,128)(2,1)S(1)}, bf16[1,2,5,16,1536]{4,3,1,2,0:T(8,128)(2,1)S(1)}, u32[]{:S(2)}, u32[]{:S(2)}) collective-permute-start(bf16[1,2,5,16,1536]{4,3,1,2,0:T(8,128)(2,1)S(1)} %get-tuple-element.100), channel_id=1, source_target_pairs={{0,2},{1,3},{2,0},{3,1},{4,6},{5,7},{6,4},{7,5},{8,10},{9,11},{10,... | collective-permute-start | bytes 1474568 | tf_op jit(solution)/shard_map/ppermute | solution.py:40
  237.7 43.4 %collective-permute-start.2 = (bf16[1,2,5,16,1536]{4,3,1,0,2:T(8,128)(2,1)S(1)}, bf16[1,2,5,16,1536]{4,3,1,0,2:T(8,128)(2,1)}, u32[]{:S(2)}, u32[]{:S(2)}) collective-permute-start(bf16[1,2,5,16,1536]{4,3,1,0,2:T(8,128)(2,1)S(1)} %get-tuple-element.99), channel_id=1, source_target_pairs={{0,3},{1,2},{2,1},{3,0},{4,7},{5,6},{6,5},{7,4},{8,11},{9,10},{10,... | collective-permute-start | bytes 1474568 | tf_op jit(solution)/shard_map/ppermute | solution.py:40
  270.4 10.7 %copy-start.6 = (bf16[1,2,5,16,1536]{4,3,1,2,0:T(8,128)(2,1)}, bf16[1,2,5,16,1536]{4,3,1,2,0:T(8,128)(2,1)S(1)}, u32[]{:S(2)}) copy-start(bf16[1,2,5,16,1536]{4,3,1,2,0:T(8,128)(2,1)S(1)} %collective-permute-done.1) | copy-start | bytes 1474564
  286.2 6.6 %copy-start.1 = (bf16[2,32,1536]{2,1,0:T(8,128)(2,1)S(1)}, bf16[2,32,1536]{2,1,0:T(8,128)(2,1)}, u32[]{:S(2)}) copy-start(bf16[2,32,1536]{2,1,0:T(8,128)(2,1)} %param.19) | copy-start | bytes 589828
Sparse Core Ops, SparseCore 0:
  9.2 27.9 all-gather.1
